TPU v7x, 256 devices: a whole 4x4x8 slice. The times are simulated.
256 devices in a mesh: dp: 16 (over z, x_lo), seq: 16 (over y, x_hi, core).
Axes of the slice: x: 4 (x_hi: 2, x_lo: 2; x = x_hi * 2 + x_lo), y: 4, z: 8, core: 2. Of those that a mesh axis runs over, the one named last changes fastest.
Arguments:
- states: bfloat16 [16, 1024, 4096], P('dp', 'seq'), may hold values from -6 to 6
- kv_weight: bfloat16 [4096, 1536], P('seq'), may hold values from -0.09375 to 0.09375
- queries: bfloat16 [16, 4096, 768], P('dp', 'seq'), may hold values from -150 to 150
- hidden: bfloat16 [16, 4096, 1536], P('dp', 'seq'), may hold values from -3 to 3
- out_proj: bfloat16 [768, 1536], P('seq'), may hold values from -0.21875 to 0.21875
- disc_in: bfloat16 [1536, 1024], replicated, may hold values from -0.15625 to 0.15625
- conv_weight: bfloat16 [41, 64, 1024], replicated, may hold values from -0.125 to 0.125
- score_weight: float32 [1024], replicated, may hold values from -0.1875 to 0.1875
- frame_len: int32 [16], replicated, may hold values from 1024 to 4096, as said below
- state_len: int32 [16], replicated, may hold values from 256 to 1024, as said below
Outputs:
- grad_out_proj: float32 [768, 1536], P('seq')
- loss_mean: float32 [], replicated
Inputs may be any that keep to these rules, and one draw needn't show every extreme that they name: `frame_len`: one clip has all 4096 frames live in every draw. `state_len`: one clip has all 1024 backbone frames live in every draw.
All inputs are finite; a program needn't handle non-finite values.
Results may differ from a plain program's by a relative error of at most 0.005.
Values may be sent and summed in bfloat16 or wider, within the bound.
No kernel may reach another device: no remote copies, remote signals or barrier semaphores. Data moves between devices by JAX's collectives and lax.ppermute only.
A program may use at most 128 MiB of HBM per device.

v0:
```python
import math
import jax
import jax.numpy as jnp
from jax import lax
from jax.sharding import PartitionSpec as P

HEAD_DIM = 128
GROUPS = 16
STRIDE = 4


def with_halo(array, sides, width):
    for axis, dim in sides:
        size, length = (lax.axis_size(axis), array.shape[dim])
        up = [(i, (i + 1) % size) for i in range(size - 1)]
        down = [(j, i) for i, j in up]
        last = lax.slice_in_dim(array, length - width, length, axis=dim)
        initial = lax.slice_in_dim(array, 0, width, axis=dim)
        before = lax.ppermute(last, axis, up)
        after = lax.ppermute(initial, axis, down)
        array = jnp.concatenate([before, array, after], axis=dim)
    return array


def regroup(weight_taps, group_count):
    kernel, group_in, channels = weight_taps.shape
    blocks = weight_taps.reshape(kernel, group_in, group_count, channels // group_count)
    turned = jnp.transpose(blocks, (0, 3, 2, 1)).reshape(kernel, channels // group_count, channels)
    return jnp.flip(turned, 0)


def disc_conv(padded, weight_taps, group_count, stride):
    return lax.conv_general_dilated(
        padded[None],
        weight_taps,
        (stride,),
        "VALID",
        dimension_numbers=("NWC", "WIO", "NWC"),
        feature_group_count=group_count,
        preferred_element_type=jnp.float32,
    )[0]


def disc_back(grad_wide, flipped, group_count, stride, high_pad):
    return lax.conv_general_dilated(
        grad_wide[None],
        flipped,
        (1,),
        [(0, high_pad)],
        lhs_dilation=(stride,),
        dimension_numbers=("NWC", "WIO", "NWC"),
        feature_group_count=group_count,
        preferred_element_type=jnp.float32,
    )[0]


def attend(query, keys_values, live_keys):
    row_count, att_width = query.shape
    head_count = att_width // HEAD_DIM
    query_heads = query.astype(jnp.float32).reshape(row_count, head_count, HEAD_DIM)
    key_heads = keys_values[:, :att_width].reshape(-1, head_count, HEAD_DIM)
    value_heads = keys_values[:, att_width:].reshape(-1, head_count, HEAD_DIM)
    scores = jnp.einsum(
        "qhd,khd->hqk", query_heads, key_heads, precision=lax.Precision.HIGHEST
    ) / math.sqrt(HEAD_DIM)
    scores = jnp.where(live_keys[None, None, :], scores, -1e30)
    row_max = jnp.max(scores, axis=2, keepdims=True)
    expo_scores = jnp.where(live_keys[None, None, :], jnp.exp(scores - row_max), 0.0)
    denom = jnp.sum(expo_scores, axis=2)
    weights = expo_scores.astype(jnp.bfloat16)
    mixed_heads = jnp.einsum(
        "hqk,khd->qhd", weights.astype(jnp.float32), value_heads, precision=lax.Precision.HIGHEST
    )
    mixed_heads = mixed_heads / jnp.transpose(denom)[:, :, None]
    return mixed_heads.reshape(row_count, att_width).astype(jnp.bfloat16)


def shards(
    states,
    kv_weight,
    queries,
    hidden,
    out_proj,
    disc_in,
    conv_weight,
    score_weight,
    frame_len,
    state_len,
):
    states_local = states[0]
    frame_count = hidden.shape[1]
    clip_index = lax.axis_index("dp")
    seq_index = lax.axis_index("seq")
    clip_pick = jnp.arange(frame_len.shape[0]) == clip_index
    clip_frames = jnp.sum(jnp.where(clip_pick, frame_len, 0))
    clip_states = jnp.sum(jnp.where(clip_pick, state_len, 0))
    sliced = states_local
    projected = jnp.dot(
        sliced,
        lax.all_gather(kv_weight, "seq", axis=0, tiled=True),
        preferred_element_type=jnp.float32,
    )
    keys_values = lax.all_gather(projected, "seq", axis=0, tiled=True)
    live_keys = jnp.arange(keys_values.shape[0]) < clip_states
    attended = attend(queries[0], keys_values, live_keys)
    sliced = attended
    lifted = hidden[0].astype(jnp.float32) + jnp.dot(
        sliced,
        lax.all_gather(out_proj, "seq", axis=0, tiled=True),
        preferred_element_type=jnp.float32,
    )
    mixed_rows = lifted.astype(jnp.bfloat16)
    frame_ids = seq_index * frame_count + jnp.arange(frame_count)
    inside = (frame_ids < clip_frames)[:, None]
    disc_feed = jnp.where(
        inside, jnp.dot(mixed_rows, disc_in, preferred_element_type=jnp.float32), 0.0
    ).astype(jnp.bfloat16)
    margin_rows = (conv_weight.shape[0] - 1) // 2
    padded = with_halo(disc_feed, (("seq", 0),), margin_rows)
    pre = disc_conv(padded, conv_weight, GROUPS, STRIDE)
    sigmoid_pre = jax.nn.sigmoid(pre)
    critic = jnp.dot(pre * sigmoid_pre, score_weight, precision=lax.Precision.HIGHEST)
    out_count = pre.shape[0]
    valid_out = STRIDE * (seq_index * out_count + jnp.arange(out_count)) < clip_frames
    shortfall = 1.0 - critic
    local_loss = jnp.sum(jnp.where(valid_out, shortfall * shortfall, 0.0))
    push_score = jnp.where(valid_out, -2.0 * shortfall, 0.0)
    slope_pre = sigmoid_pre * (1.0 + pre * (1.0 - sigmoid_pre))
    grad_pre = (push_score[:, None] * score_weight[None, :] * slope_pre).astype(jnp.bfloat16)
    reach_out = margin_rows // STRIDE
    grad_wide = with_halo(grad_pre, (("seq", 0),), reach_out)
    grad_feed = disc_back(grad_wide, regroup(conv_weight, GROUPS), GROUPS, STRIDE, STRIDE - 1)
    grad_feed = jnp.where(inside, grad_feed, 0.0).astype(jnp.bfloat16)
    grad_mixed = lax.dot_general(
        grad_feed, disc_in, (((1,), (1,)), ((), ())), preferred_element_type=jnp.float32
    ).astype(jnp.bfloat16)
    full_term = lax.dot_general(
        attended, grad_mixed, (((0,), (0,)), ((), ())), preferred_element_type=jnp.float32
    )
    summed_clips = lax.psum(full_term, "dp")
    grad_proj = lax.psum_scatter(summed_clips, "seq", scatter_dimension=0, tiled=True)
    total_loss = lax.psum(local_loss, ("dp", "seq"))
    counted = jnp.sum((frame_len + STRIDE - 1) // STRIDE).astype(jnp.float32)
    return (grad_proj, total_loss / counted)


def solution(mesh):
    return jax.shard_map(
        shards,
        mesh=mesh,
        in_specs=(
            P("dp", "seq", None),
            P("seq", None),
            P("dp", "seq", None),
            P("dp", "seq", None),
            P("seq", None),
            P(),
            P(),
            P(),
            P(),
            P(),
        ),
        out_specs=(P("seq", None), P()),
        check_vma=False,
    )
```

profile of v0, /device:TPU:8, one launch (start us, length us, event | category | flops | bytes accessed | tf_op | source)
XLA Modules:
  0.0 666.0 jit_solution(14477105413284666974)
XLA Ops:
  8.0 100.1 %all-gather.4.cloned.1.call-done = bf16[4096,1536]{1,0:T(8,128)(2,1)} async-done(((bf16[256,1536]{1,0:T(8,128)(2,1)}), bf16[4096,1536]{1,0:T(8,128)(2,1)}) %all-gather.4.cloned.1.call-update) | async-done | bytes 12582928 | tf_op jit(solution)/shard_map/all_gather | solution.py:100
  108.1 7.8 %fusion.31 = f32[64,1536]{1,0:T(8,128)} fusion(bf16[4096,1536]{1,0:T(8,128)(2,1)} %all-gather.4.cloned.1.call-done, bf16[1,64,4096]{2,1,0:T(8,128)(2,1)} %param.10), kind=kOutput, calls=%fused_computation.30 | convolution fusion | flops 805306368 | bytes 13500416 | tf_op jit(solution)/shard_map/dot_general | solution.py:98
  119.9 63.1 %all-gather.6.cloned.1.call-done = f32[1024,1536]{1,0:T(8,128)} async-done(((f32[64,1536]{1,0:T(8,128)}), f32[1024,1536]{1,0:T(8,128)}) %all-gather.6.cloned.1.call-update) | async-done | bytes 6291472 | tf_op jit(solution)/shard_map/all_gather | solution.py:103
  183.0 5.9 fusion.48
  188.9 3.5 copy.19
  192.5 3.6 copy.18
  196.0 4.6 fusion.52
  200.6 2.4 fusion.51
  203.1 1.7 fusion.24
  204.8 33.3 %all-gather.8.cloned.1.call-done = bf16[768,1536]{1,0:T(8,128)(2,1)} async-done(((bf16[48,1536]{1,0:T(8,128)(2,1)}), bf16[768,1536]{1,0:T(8,128)(2,1)}) %all-gather.8.cloned.1.call-update) | async-done | bytes 2359312 | tf_op jit(solution)/shard_map/all_gather | solution.py:109
  238.1 4.3 fusion.23
  243.8 2.2 collective-permute-start
  246.0 5.8 collective-permute-start.1
  251.8 14.8 %shard_map.115 = bf16[41,64,16,64]{3,2,1,0:T(8,128)(2,1)} reshape(bf16[41,64,1024]{2,1,0:T(8,128)(2,1)} %param.16) | data formatting | bytes 10747904 | tf_op jit(solution)/shard_map/shard_map
  266.6 2.0 pad_maximum_fusion
  268.6 2.3 copy.24
  270.9 6.3 copy.25
  277.2 18.9 %fusion.27 = f32[64,16,64]{2,1,0:T(8,128)} fusion(bf16[1,296,16,64]{3,0,2,1:T(2,128)(2,1)} %copy.25, bf16[41,64,16,64]{3,2,1,0:T(8,128)(2,1)} %shard_map.115), kind=kOutput, calls=%fused_computation.25 | convolution fusion | flops 343932928 | bytes 6242304 | tf_op jit(solution)/shard_map/conv_general_dilated | solution.py:33
  299.1 1.9 collective-permute-start.2
  301.0 6.0 collective-permute-start.3
  307.1 19.1 %copy.27 = bf16[41,64,16,64]{1,2,3,0:T(8,128)(2,1)} copy(bf16[41,64,16,64]{3,2,1,0:T(8,128)(2,1)} %shard_map.115) | data formatting | bytes 10747904 | tf_op jit(solution)/shard_map/shard_map
  326.2 15.0 %reshape.48 = bf16[41,64,1024]{2,1,0:T(8,128)(2,1)} reshape(bf16[41,64,16,64]{3,2,1,0:T(8,128)(2,1)} %bitcast.55) | data formatting | bytes 10747904 | tf_op jit(solution)/shard_map/reshape | solution.py:28
  341.2 5.9 rev.6
  347.1 14.8 %rev.7 = bf16[41,64,16,64]{3,2,1,0:T(8,128)(2,1)} reshape(bf16[41,64,1024]{2,1,0:T(8,128)(2,1)} %rev.6) | data formatting | bytes 10747904 | tf_op jit(solution)/shard_map/jit(_flip)/rev | solution.py:29
  363.2 54.6 %fusion.1 = bf16[1,256,16,64]{3,0,2,1:T(2,128)(2,1)} fusion(bf16[1,74,16,64]{3,0,2,1:T(2,128)(2,1)} %broadcast_in_dim.69, bf16[41,64,16,64]{3,2,1,0:T(8,128)(2,1)} %rev.7), kind=kOutput, calls=%fused_computation.1 | convolution fusion | flops 343932928 | bytes 6049792 | tf_op jit(solution)/shard_map/conv_general_dilated | solution.py:45
  417.8 5.7 copy.30
  423.5 2.1 copy.31
  425.5 4.8 fusion.16
  430.4 88.9 %reduce-scatter.2.cloned.1.call-done = f32[48,1536]{1,0:T(8,128)} async-done(((f32[768,1536]{1,0:T(8,128)}), f32[48,1536]{1,0:T(8,128)}) %reduce-scatter.2.cloned.1.call-update) | async-done | bytes 294928 | tf_op jit(solution)/shard_map/reduce_scatter | solution.py:141
  520.0 74.0 %psum.15 = f32[]{:T(128)} all-reduce(f32[]{:T(128)} %get-tuple-element.10), channel_id=1, replica_groups=mesh['dp'=16,'seq'=16] {'dp','seq'}, use_global_device_ids=true, to_apply=%region_7.8 | all-reduce | flops 1 | bytes 8 | tf_op jit(solution)/shard_map/psum | solution.py:142
  594.7 61.6 %all-reduce.2.cloned.1.call-done = f32[48,1536]{1,0:T(8,128)} async-done(((f32[48,1536]{1,0:T(8,128)}), f32[48,1536]{1,0:T(8,128)}) %all-reduce.2.cloned.1.call-update) | async-done | bytes 294928 | tf_op jit(solution)/shard_map/psum | solution.py:140
  656.3 1.7 copy.42
  (43 shorter events, 10.5 us)
Async XLA Ops:
  7.2 231.0 %copy-start = (bf16[1536,1024]{1,0:T(8,128)(2,1)S(1)}, bf16[1536,1024]{1,0:T(8,128)(2,1)}, u32[]{:S(2)}) copy-start(bf16[1536,1024]{1,0:T(8,128)(2,1)} %param.15) | copy-start | bytes 9437188
  7.2 100.9 %all-gather.4.cloned.1.call-start = ((), (), s32[]{:S(2)}) async-start(), calls=%async_computation.1 | async-start | bytes 13369344 | tf_op jit(solution)/shard_map/all_gather | solution.py:100
  7.9 109.9 %copy-start.7 = (s32[16]{0:T(128)S(1)}, s32[16]{0:T(128)}, u32[]{:S(2)}) copy-start(s32[16]{0:T(128)} %param.18) | copy-start | bytes 196
  7.9 109.9 %copy-start.8 = (s32[16]{0:T(128)S(1)}, s32[16]{0:T(128)}, u32[]{:S(2)}) copy-start(s32[16]{0:T(128)} %param.19) | copy-start | bytes 196
  7.9 175.1 %all-gather.6.cloned.1.call-start = ((), (), s32[]{:S(2)}) async-start(), calls=%async_computation.2 | async-start | bytes 6684672 | tf_op jit(solution)/shard_map/all_gather | solution.py:103
  115.9 122.3 %all-gather.8.cloned.1.call-start = ((), (), s32[]{:S(2)}) async-start(), calls=%async_computation.3 | async-start | bytes 2506752 | tf_op jit(solution)/shard_map/all_gather | solution.py:109
  116.6 402.7 %reduce-scatter.2.cloned.1.call-start = ((), (), s32[]{:S(2)}) async-start(), calls=%async_computation.4 | async-start | bytes 5013504 | tf_op jit(solution)/shard_map/reduce_scatter | solution.py:141
  119.2 118.9 %copy-start.5 = (pred[256]{0:T(512)(128)(4,1)}, pred[256]{0:T(512)(128)(4,1)S(1)}, u32[]{:S(2)}) copy-start(pred[256]{0:T(512)(128)(4,1)S(1)} %add_compare_fusion) | copy-start | bytes 772
  200.6 2.4 copy-start.1
  204.8 37.6 %copy-start.2 = (bf16[256,6,128]{0,2,1:T(8,128)(2,1)}, bf16[256,6,128]{0,2,1:T(8,128)(2,1)S(1)}, u32[]{:S(2)}) copy-start(bf16[256,6,128]{0,2,1:T(8,128)(2,1)S(1)} %fusion.24) | copy-start | bytes 1179652
  243.8 22.7 %collective-permute-start = (bf16[20,1024]{1,0:T(8,128)(2,1)}, bf16[20,1024]{1,0:T(8,128)(2,1)S(1)}, u32[]{:S(2)}, u32[]{:S(2)}) collective-permute-start(bf16[20,1024]{1,0:T(8,128)(2,1)} %get-tuple-element.6), channel_id=1, source_target_pairs={{0,1},{1,2},{2,3},{3,4},{4,5},{5,6},{6,7},{7,8},{8,9},{9,10},{10,1... | collective-permute-start | bytes 122888 | tf_op jit(solution)/shard_map/ppermute | solution.py:19
  246.0 20.6 %collective-permute-start.1 = (bf16[20,1024]{1,0:T(8,128)(2,1)}, bf16[20,1024]{1,0:T(8,128)(2,1)S(1)}, u32[]{:S(2)}, u32[]{:S(2)}) collective-permute-start(bf16[20,1024]{1,0:T(8,128)(2,1)} %get-tuple-element.7), channel_id=1, source_target_pairs={{1,0},{2,1},{3,2},{4,3},{5,4},{6,5},{7,6},{8,7},{9,8},{10,9},{11,1... | collective-permute-start | bytes 122888 | tf_op jit(solution)/shard_map/ppermute | solution.py:20
  277.2 20.1 %copy-start.4 = (f32[1024]{0:T(1024)S(1)}, f32[1024]{0:T(1024)}, u32[]{:S(2)}) copy-start(f32[1024]{0:T(1024)} %param.17) | copy-start | bytes 12292
  299.1 62.8 %collective-permute-start.2 = (bf16[5,1024]{1,0:T(8,128)(2,1)S(1)}, bf16[5,1024]{1,0:T(8,128)(2,1)S(1)}, u32[]{:S(2)}, u32[]{:S(2)}) collective-permute-start(bf16[5,1024]{1,0:T(8,128)(2,1)S(1)} %get-tuple-element.8), channel_id=1, source_target_pairs={{0,1},{1,2},{2,3},{3,4},{4,5},{5,6},{6,7},{7,8},{8,9},{9,10},{10,1... | collective-permute-start | bytes 30728 | tf_op jit(solution)/shard_map/ppermute | solution.py:19
  301.0 60.9 %collective-permute-start.3 = (bf16[5,1024]{1,0:T(8,128)(2,1)S(1)}, bf16[5,1024]{1,0:T(8,128)(2,1)S(1)}, u32[]{:S(2)}, u32[]{:S(2)}) collective-permute-start(bf16[5,1024]{1,0:T(8,128)(2,1)S(1)} %get-tuple-element.9), channel_id=1, source_target_pairs={{1,0},{2,1},{3,2},{4,3},{5,4},{6,5},{7,6},{8,7},{9,8},{10,9},{11,1... | collective-permute-start | bytes 30728 | tf_op jit(solution)/shard_map/ppermute | solution.py:20
  417.8 7.7 %copy-start.3 = (bf16[256,6,128]{0,2,1:T(8,128)(2,1)S(1)}, bf16[256,6,128]{0,2,1:T(8,128)(2,1)}, u32[]{:S(2)}) copy-start(bf16[256,6,128]{0,2,1:T(8,128)(2,1)} %copy-done.2) | copy-start | bytes 1179652
  417.8 7.7 %copy-start.6 = (pred[256]{0:T(512)(128)(4,1)S(1)}, pred[256]{0:T(512)(128)(4,1)}, u32[]{:S(2)}) copy-start(pred[256]{0:T(512)(128)(4,1)} %copy-done.5) | copy-start | bytes 772
  430.4 225.9 %all-reduce.2.cloned.1.call-start = ((), (), s32[]{:S(2)}) async-start(), calls=%async_computation.5 | async-start | bytes 589824 | tf_op jit(solution)/shard_map/psum | solution.py:140
Sparse Core Ops, SparseCore 0:
  10.8 97.2 all-gather.3
  116.0 66.9 all-gather.5
  185.8 52.2 all-gather.7
  430.5 88.7 reduce-scatter.1
  522.0 134.2 all-reduce.1
where the time goes:
time: 678 us; the launch traced here: 666 us
  waiting for transfers between devices  348 us (51%)
  local copies, waits for them, and re-layouts  106 us (16%)
  matrix products  98.3 us (14%)
  blocking collectives  74 us (11%)
  between operations  16.8 us (2%)
  starting transfers between devices  16.1 us (2%)
    all_gather x1, waiting for transfers between devices, shards(): lax.all_gather(kv_weight, 'seq', axis=0, tiled=True)  100 us
    reduce_scatter x1, waiting for transfers between devices, shards(): lax.psum_scatter(summed_clips, 'seq', scatter_dimension=0, tiled=True)  88.9 us
    psum x1, blocking collectives, shards(): total_loss = lax.psum(local_loss, ('dp', 'seq'))  74 us
    all_gather x1, waiting for transfers between devices, shards(): keys_values = lax.all_gather(projected, 'seq', axis=0, tiled=True)  63.1 us
    psum x1, waiting for transfers between devices, shards(): summed_clips = lax.psum(full_term, 'dp')  61.6 us
    conv_general_dilated x1, matrix products, disc_back(): lax.conv_general_dilated(grad_wide[None], flipped, (1,), [(0, high_pad)],...  54.6 us
    another operation x2, local copies, waits for them, and re-layouts  33.9 us
    all_gather x1, waiting for transfers between devices, shards(): lax.all_gather(out_proj, 'seq', axis=0, tiled=True)  33.3 us
  transfers between devices with their start and end apart: 9, of which 5 were waited for; matrix products, arithmetic and copies ran while one was open for 14% of the time, Pallas kernels for 0%

commit v1 on v0

--- a/solution.py
+++ b/solution.py
@@ -137,7 +137,7 @@
     full_term = lax.dot_general(
         attended, grad_mixed, (((0,), (0,)), ((), ())), preferred_element_type=jnp.float32
     )
-    summed_clips = lax.psum(full_term, "dp")
+    summed_clips = jnp.sum(lax.all_gather(full_term, "dp"), axis=0)
     grad_proj = lax.psum_scatter(summed_clips, "seq", scatter_dimension=0, tiled=True)
     total_loss = lax.psum(local_loss, ("dp", "seq"))
     counted = jnp.sum((frame_len + STRIDE - 1) // STRIDE).astype(jnp.float32)

time: 678 us -> 2100 us (3.10)
  waiting for transfers between devices: 348 us -> 1740 us
  other arithmetic: 6.65 us -> 32.7 us
    all_gather x0 -> x1, waiting for transfers between devices: none -> 1530 us  [shards(): summed_clips = jnp.sum(lax.all_gather(full_term, 'dp'), axis=0)]
    reduce_scatter x1, waiting for transfers between devices: 88.9 us -> 14.4 us  [shards(): lax.psum_scatter(summed_clips, 'seq', scatter_dimension=0, tiled=True)]
    psum x1 -> x0, waiting for transfers between devices: 61.6 us -> none  [shards(): summed_clips = lax.psum(full_term, 'dp')]
    reduce_sum x0 -> x1, other arithmetic: none -> 26 us  [shards(): summed_clips = jnp.sum(lax.all_gather(full_term, 'dp'), axis=0)]
  transfers between devices with their start and end apart: 9 -> 9, of which waited for: 5 -> 5; matrix products, arithmetic and copies ran while one was open for 14% -> 5% of each run, Pallas kernels for 0% -> 0%
where the time goes in v1:
time: 2100 us; the launch traced here: 2090 us
  waiting for transfers between devices  1740 us (83%)
  local copies, waits for them, and re-layouts  104 us (5%)
  matrix products  98.3 us (5%)
  blocking collectives  75.6 us (4%)
  other arithmetic  32.7 us (2%)
    all_gather x1, waiting for transfers between devices, shards(): summed_clips = jnp.sum(lax.all_gather(full_term, 'dp'), axis=0)  1530 us
    all_gather x1, waiting for transfers between devices, shards(): lax.all_gather(kv_weight, 'seq', axis=0, tiled=True)  100 us
    psum x1, blocking collectives, shards(): total_loss = lax.psum(local_loss, ('dp', 'seq'))  75.6 us
    all_gather x1, waiting for transfers between devices, shards(): keys_values = lax.all_gather(projected, 'seq', axis=0, tiled=True)  63.1 us
    conv_general_dilated x1, matrix products, disc_back(): lax.conv_general_dilated(grad_wide[None], flipped, (1,), [(0, high_pad)],...  54.6 us
  transfers between devices with their start and end apart: 9, of which 5 were waited for; matrix products, arithmetic and copies ran while one was open for 5% of the time, Pallas kernels for 0%

profile of v1, /device:TPU:8, one launch (start us, length us, event | category | flops | bytes accessed | tf_op | source)
XLA Modules:
  0.0 2085.2 jit_solution(12646026438519398275)
XLA Ops:
  8.0 100.1 %all-gather.6.cloned.1.call-done = bf16[4096,1536]{1,0:T(8,128)(2,1)} async-done(((bf16[256,1536]{1,0:T(8,128)(2,1)}), bf16[4096,1536]{1,0:T(8,128)(2,1)}) %all-gather.6.cloned.1.call-update) | async-done | bytes 12582928 | tf_op jit(solution)/shard_map/all_gather | solution.py:100
  108.1 7.8 fusion.31
  119.9 63.1 %all-gather.8.cloned.1.call-done = f32[1024,1536]{1,0:T(8,128)} async-done(((f32[64,1536]{1,0:T(8,128)}), f32[1024,1536]{1,0:T(8,128)}) %all-gather.8.cloned.1.call-update) | async-done | bytes 6291472 | tf_op jit(solution)/shard_map/all_gather | solution.py:103
  183.0 5.9 fusion.48
  188.9 3.5 copy.19
  192.5 3.6 copy.18
  196.0 4.6 fusion.52
  200.6 2.4 fusion.51
  203.1 1.7 fusion.24
  204.8 33.3 %all-gather.10.cloned.1.call-done = bf16[768,1536]{1,0:T(8,128)(2,1)} async-done(((bf16[48,1536]{1,0:T(8,128)(2,1)}), bf16[768,1536]{1,0:T(8,128)(2,1)}) %all-gather.10.cloned.1.call-update) | async-done | bytes 2359312 | tf_op jit(solution)/shard_map/all_gather | solution.py:109
  238.1 4.3 fusion.23
  243.8 2.2 collective-permute-start
  246.0 5.8 collective-permute-start.1
  251.8 14.8 shard_map.115
  266.6 2.0 pad_maximum_fusion
  268.6 2.3 copy.24
  270.9 6.3 copy.25
  277.2 18.9 fusion.27
  299.1 1.9 collective-permute-start.2
  301.0 6.0 collective-permute-start.3
  307.1 19.1 copy.27
  326.2 15.0 reshape.48
  341.2 5.9 rev.6
  347.1 14.8 rev.7
  363.2 54.6 %fusion.1 = bf16[1,256,16,64]{3,0,2,1:T(2,128)(2,1)} fusion(bf16[1,74,16,64]{3,0,2,1:T(2,128)(2,1)} %broadcast_in_dim.69, bf16[41,64,16,64]{3,2,1,0:T(8,128)(2,1)} %rev.7), kind=kOutput, calls=%fused_computation.1 | convolution fusion | flops 343932928 | bytes 6049792 | tf_op jit(solution)/shard_map/conv_general_dilated | solution.py:45
  417.8 5.7 copy.30
  423.5 2.0 copy.31
  425.5 4.9 fusion.16
  430.5 1529.4 %all-gather.12.cloned.1.call-done = f32[12288,1536]{1,0:T(8,128)} async-done(((f32[768,1536]{1,0:T(8,128)}), f32[12288,1536]{1,0:T(8,128)}) %all-gather.12.cloned.1.call-update) | async-done | bytes 75497488 | tf_op jit(solution)/shard_map/all_gather | solution.py:140
  1959.8 26.0 %reduce_sum.57 = f32[768,1536]{1,0:T(8,128)} reduce(f32[16,768,1536]{2,1,0:T(8,128)} %bitcast.14, f32[]{:T(128)} %constant.42.clone.1), dimensions={0}, to_apply=%region_4.5 | reduce | flops 17694720 | bytes 80216064 | tf_op jit(solution)/shard_map/reduce_sum | solution.py:140
  1986.6 75.6 %psum.7 = f32[]{:T(128)} all-reduce(f32[]{:T(128)} %get-tuple-element.10), channel_id=1, replica_groups=mesh['dp'=16,'seq'=16] {'dp','seq'}, use_global_device_ids=true, to_apply=%region_7.8 | all-reduce | flops 1 | bytes 8 | tf_op jit(solution)/shard_map/psum | solution.py:142
  2062.8 14.4 reduce-scatter.2.cloned.1.call-done
  (43 shorter events, 10.5 us)
Async XLA Ops:
  7.2 231.0 %copy-start = (bf16[1536,1024]{1,0:T(8,128)(2,1)S(1)}, bf16[1536,1024]{1,0:T(8,128)(2,1)}, u32[]{:S(2)}) copy-start(bf16[1536,1024]{1,0:T(8,128)(2,1)} %param.15) | copy-start | bytes 9437188
  7.2 100.9 %all-gather.6.cloned.1.call-start = ((), (), s32[]{:S(2)}) async-start(), calls=%async_computation.1 | async-start | bytes 13369344 | tf_op jit(solution)/shard_map/all_gather | solution.py:100
  7.9 109.9 %copy-start.7 = (s32[16]{0:T(128)S(1)}, s32[16]{0:T(128)}, u32[]{:S(2)}) copy-start(s32[16]{0:T(128)} %param.18) | copy-start | bytes 196
  7.9 109.9 %copy-start.8 = (s32[16]{0:T(128)S(1)}, s32[16]{0:T(128)}, u32[]{:S(2)}) copy-start(s32[16]{0:T(128)} %param.19) | copy-start | bytes 196
  7.9 175.1 %all-gather.8.cloned.1.call-start = ((), (), s32[]{:S(2)}) async-start(), calls=%async_computation.2 | async-start | bytes 6684672 | tf_op jit(solution)/shard_map/all_gather | solution.py:103
  115.9 122.3 %all-gather.10.cloned.1.call-start = ((), (), s32[]{:S(2)}) async-start(), calls=%async_computation.3 | async-start | bytes 2506752 | tf_op jit(solution)/shard_map/all_gather | solution.py:109
  116.6 1843.2 %all-gather.12.cloned.1.call-start = ((), (), s32[]{:S(2)}) async-start(), calls=%async_computation.5 | async-start | bytes 80216064 | tf_op jit(solution)/shard_map/all_gather | solution.py:140
  119.2 118.9 %copy-start.5 = (pred[256]{0:T(512)(128)(4,1)}, pred[256]{0:T(512)(128)(4,1)S(1)}, u32[]{:S(2)}) copy-start(pred[256]{0:T(512)(128)(4,1)S(1)} %add_compare_fusion) | copy-start | bytes 772
  200.6 2.4 copy-start.1
  204.8 37.6 %copy-start.2 = (bf16[256,6,128]{0,2,1:T(8,128)(2,1)}, bf16[256,6,128]{0,2,1:T(8,128)(2,1)S(1)}, u32[]{:S(2)}) copy-start(bf16[256,6,128]{0,2,1:T(8,128)(2,1)S(1)} %fusion.24) | copy-start | bytes 1179652
  243.8 22.7 %collective-permute-start = (bf16[20,1024]{1,0:T(8,128)(2,1)}, bf16[20,1024]{1,0:T(8,128)(2,1)S(1)}, u32[]{:S(2)}, u32[]{:S(2)}) collective-permute-start(bf16[20,1024]{1,0:T(8,128)(2,1)} %get-tuple-element.6), channel_id=1, source_target_pairs={{0,1},{1,2},{2,3},{3,4},{4,5},{5,6},{6,7},{7,8},{8,9},{9,10},{10,1... | collective-permute-start | bytes 122888 | tf_op jit(solution)/shard_map/ppermute | solution.py:19
  246.0 20.6 collective-permute-start.1
  277.2 20.1 copy-start.4
  299.1 62.8 %collective-permute-start.2 = (bf16[5,1024]{1,0:T(8,128)(2,1)S(1)}, bf16[5,1024]{1,0:T(8,128)(2,1)S(1)}, u32[]{:S(2)}, u32[]{:S(2)}) collective-permute-start(bf16[5,1024]{1,0:T(8,128)(2,1)S(1)} %get-tuple-element.8), channel_id=1, source_target_pairs={{0,1},{1,2},{2,3},{3,4},{4,5},{5,6},{6,7},{7,8},{8,9},{9,10},{10,1... | collective-permute-start | bytes 30728 | tf_op jit(solution)/shard_map/ppermute | solution.py:19
  301.0 60.9 %collective-permute-start.3 = (bf16[5,1024]{1,0:T(8,128)(2,1)S(1)}, bf16[5,1024]{1,0:T(8,128)(2,1)S(1)}, u32[]{:S(2)}, u32[]{:S(2)}) collective-permute-start(bf16[5,1024]{1,0:T(8,128)(2,1)S(1)} %get-tuple-element.9), channel_id=1, source_target_pairs={{1,0},{2,1},{3,2},{4,3},{5,4},{6,5},{7,6},{8,7},{9,8},{10,9},{11,1... | collective-permute-start | bytes 30728 | tf_op jit(solution)/shard_map/ppermute | solution.py:20
  417.8 7.7 copy-start.3
  417.8 7.7 copy-start.6
  430.4 1646.8 %reduce-scatter.2.cloned.1.call-start = ((), (), s32[]{:S(2)}) async-start(), calls=%async_computation.4 | async-start | bytes 5013504 | tf_op jit(solution)/shard_map/reduce_scatter | solution.py:141
Sparse Core Ops, SparseCore 0:
  10.8 97.2 all-gather.5
  116.0 66.9 all-gather.7
  185.8 52.2 all-gather.9
  430.5 1529.2 all-gather.11
  1986.0 91.0 reduce-scatter.1
